TPU v7x, 512 devices: a whole 4x4x16 slice. The times are simulated.
512 devices in a mesh: coef: 16 (over z_lo, y), pair: 32 (over z_hi, x, core).
Axes of the slice: x: 4, y: 4, z: 16 (z_hi: 4, z_lo: 4; z = z_hi * 4 + z_lo), core: 2. Of those that a mesh axis runs over, the one named last changes fastest.
Arguments:
- integrals: bfloat16 [2048, 32, 8192], P(('coef', 'pair')), may hold values from -66 to 66
- coefficients: bfloat16 [2, 8192, 384], P(None, ('coef', 'pair')), may hold values from -0.0625 to 0.0625
- shell_starts: int32 [8], replicated, may hold values from 0 to 8188, as said below
- pair_ids: int32 [16, 128], P('coef'), may hold values from 0 to 127, each once within a row
Outputs:
- half_ints: bfloat16 [2, 384, 384, 2048], P(None, 'pair', None, 'coef')
Inputs may be any that keep to these rules, and one draw needn't show every extreme that they name: `shell_starts`: distinct multiples of 4.
All inputs are finite; a program needn't handle non-finite values.
Results may differ from a plain program's by a relative error of at most 0.0049.
Values may be sent and summed in bfloat16 or wider, within the bound.
A program may use at most 64 MiB of HBM per device.

v0:
```python
import jax
import jax.numpy as jnp
from jax import lax
from jax.sharding import PartitionSpec as P

SHW = 4


def on_device(integrals, coefficients, shell_starts, pair_ids):
    slot_count, batch_rows, ao_width = integrals.shape
    occupied = coefficients.shape[2]
    flat_ints = integrals.reshape(slot_count * batch_rows, ao_width)
    offsets = jnp.arange(SHW, dtype=jnp.int32)
    batch_index = (shell_starts[:, None] + offsets[None, :]).reshape(-1)
    panel_piece = lax.all_gather(coefficients, ("coef", "pair"), axis=1, tiled=True)
    products = jnp.einsum("rn,cnj->crj", flat_ints, panel_piece, preferred_element_type=jnp.float32)
    row_count = panel_piece.shape[1]
    inside_mask = (batch_index >= 0) & (batch_index < row_count)
    safe_index = jnp.clip(batch_index, 0, row_count - 1)
    chosen = jnp.take(panel_piece, safe_index, axis=1).astype(jnp.float32)
    picked = jnp.where(inside_mask[None, :, None], chosen, 0.0)
    half_done, picked = (products, picked)
    batch_coef = picked.astype(jnp.bfloat16)
    half_done = half_done.astype(jnp.bfloat16).reshape(2, slot_count, batch_rows, occupied)
    real_part = jnp.einsum(
        "mi,kmj->kij", batch_coef[0], half_done[0], preferred_element_type=jnp.float32
    ) + jnp.einsum("mi,kmj->kij", batch_coef[1], half_done[1], preferred_element_type=jnp.float32)
    imag_part = jnp.einsum(
        "mi,kmj->kij", batch_coef[0], half_done[1], preferred_element_type=jnp.float32
    ) - jnp.einsum("mi,kmj->kij", batch_coef[1], half_done[0], preferred_element_type=jnp.float32)
    local_block = jnp.stack([real_part, imag_part]).astype(jnp.bfloat16)
    arrived = lax.all_to_all(local_block, "pair", split_axis=2, concat_axis=1, tiled=True)
    pair_order = pair_ids.reshape(-1)
    columns = jnp.arange(pair_order.shape[0], dtype=jnp.int32)
    selector = (pair_order[:, None] == columns[None, :]).astype(jnp.bfloat16)
    result = jnp.einsum("csij,sq->cijq", arrived, selector, preferred_element_type=jnp.float32)
    return result.astype(jnp.bfloat16)


def solution(mesh):
    return jax.shard_map(
        on_device,
        mesh=mesh,
        in_specs=(
            P(("coef", "pair"), None, None),
            P(None, ("coef", "pair"), None),
            P(),
            P("coef", None),
        ),
        out_specs=P(None, "pair", None, "coef"),
        check_vma=False,
    )
```

profile of v0, /device:TPU:97, one launch (start us, length us, event | category | flops | bytes accessed | tf_op | source)
XLA Modules:
  0.0 1120.1 jit_solution(15795770854735174628)
XLA Ops:
  6.5 0.0 copy-start
  6.5 0.0 all-gather.2.cloned.1.call-start
  6.5 0.7 all-gather.2.cloned.1.call-update
  7.3 0.7 fusion.14
  8.0 0.1 min.18
  8.1 0.1 min.16
  8.1 0.7 fusion.17
  8.9 0.1 and.18
  9.0 832.1 %all-gather.2.cloned.1.call-done = bf16[2,8192,384]{2,1,0:T(8,128)(2,1)} async-done(((bf16[2,16,384]{2,1,0:T(8,128)(2,1)}), bf16[2,8192,384]{2,1,0:T(8,128)(2,1)}) %all-gather.2.cloned.1.call-update) | async-done | bytes 12582928 | tf_op jit(solution)/shard_map/all_gather | solution.py:15
  841.1 0.0 copy-done
  841.1 6.5 fusion.7
  847.7 1.6 copy-done.1
  849.3 117.8 %copy.11 = bf16[2,8192,384]{2,0,1:T(2,128)(2,1)} copy(bf16[2,8192,384]{2,1,0:T(8,128)(2,1)S(1)} %copy-done.1) | data formatting | bytes 25165824 | tf_op jit(solution)/shard_map/all_gather | solution.py:15
  967.0 5.2 gather_fusion
  972.3 0.1 fusion.10
  972.4 0.5 fusion.13
  972.9 0.5 fusion.12
  973.4 0.5 fusion.5
  973.9 0.5 fusion.6
  974.4 1.7 pad_maximum_fusion
  976.1 5.4 copy.13
  981.5 127.7 %all_to_all.18 = bf16[2,4,384,384]{3,1,0,2:T(4,128)(2,1)S(1)} all-to-all(bf16[2,4,384,384]{3,1,0,2:T(4,128)(2,1)} %copy.13), channel_id=1, replica_groups=mesh['coef'=16,'pair'=32] {'pair'}, dimensions={2} | all-to-all | bytes 4718592 | tf_op jit(solution)/shard_map/all_to_all | solution.py:32
  1109.2 1.8 copy.15
  1111.0 2.3 fusion.2
  (7 shorter events, 0.0 us)
Async XLA Ops:
  6.5 834.6 %copy-start = (bf16[4,32,8192]{2,1,0:T(8,128)(2,1)S(1)}, bf16[4,32,8192]{2,1,0:T(8,128)(2,1)}, u32[]{:S(2)}) copy-start(bf16[4,32,8192]{2,1,0:T(8,128)(2,1)} %param.4) | copy-start | bytes 6291460
  6.5 834.6 %all-gather.2.cloned.1.call-start = ((), (), s32[]{:S(2)}) async-start(), calls=%async_computation.1 | async-start | bytes 12607488 | tf_op jit(solution)/shard_map/all_gather | solution.py:15
  841.1 8.2 copy-start.1
  1109.1 1.8 copy-start.2
Sparse Core Ops, SparseCore 0:
  9.5 831.5 all-gather.1
where the time goes:
time: 1120 us
  waiting for transfers between devices  833 us (74%)
  local copies, waits for them, and re-layouts  132 us (12%)
  blocking collectives  128 us (11%)
  between operations  13.5 us (1%)
    all_gather x1, waiting for transfers between devices, on_device(): lax.all_gather(coefficients, ('coef', 'pair'), axis=1, tiled=True)  832 us
    all_to_all x1, blocking collectives, on_device(): lax.all_to_all(local_block, 'pair', split_axis=2, concat_axis=1, tiled=True)  128 us
    all_gather x1, local copies, waits for them, and re-layouts, on_device(): lax.all_gather(coefficients, ('coef', 'pair'), axis=1, tiled=True)  118 us
  transfers between devices with their start and end apart: 1, of which 1 were waited for; matrix products, arithmetic and copies ran while one was open for 0% of the time, Pallas kernels for 0%

commit v1 on v0

--- a/solution.py
+++ b/solution.py
@@ -12,7 +12,12 @@
     flat_ints = integrals.reshape(slot_count * batch_rows, ao_width)
     offsets = jnp.arange(SHW, dtype=jnp.int32)
     batch_index = (shell_starts[:, None] + offsets[None, :]).reshape(-1)
-    panel_piece = lax.all_gather(coefficients, ("coef", "pair"), axis=1, tiled=True)
+    panel_piece = jnp.concatenate(
+        lax.all_to_all(
+            jnp.stack([coefficients] * lax.axis_size(("coef", "pair"))), ("coef", "pair"), 0, 0
+        ),
+        axis=1,
+    )
     products = jnp.einsum("rn,cnj->crj", flat_ints, panel_piece, preferred_element_type=jnp.float32)
     row_count = panel_piece.shape[1]
     inside_mask = (batch_index >= 0) & (batch_index < row_count)

time: 1120 us -> 844 us (0.75)
  the two profiles are of different devices: /device:TPU:97 before, /device:TPU:33 now
where the time goes in v1:
time: 844 us; the launch traced here: 843 us
  waiting for transfers between devices  541 us (64%)
  local copies, waits for them, and re-layouts  144 us (17%)
  blocking collectives  125 us (15%)
  starting transfers between devices  25.1 us (3%)
    all_to_all x1, waiting for transfers between devices, on_device(): lax.all_to_all(jnp.stack([coefficients] * lax.axis_size(('coef', 'pair'))...  541 us
    reshape x2, local copies, waits for them, and re-layouts, on_device(): jnp.concatenate(lax.all_to_all(jnp.stack([coefficients] * lax.axis_size((...  125 us
    all_to_all x1, blocking collectives, on_device(): lax.all_to_all(local_block, 'pair', split_axis=2, concat_axis=1, tiled=True)  125 us
    all_to_all x1, starting transfers between devices, on_device(): lax.all_to_all(jnp.stack([coefficients] * lax.axis_size(('coef', 'pair'))...  25.1 us
  transfers between devices with their start and end apart: 1, of which 1 were waited for; matrix products, arithmetic and copies ran while one was open for 0% of the time, Pallas kernels for 0%

profile of v1, /device:TPU:33, one launch (start us, length us, event | category | flops | bytes accessed | tf_op | source)
XLA Modules:
  0.0 843.2 jit_solution(5279647766179504817)
XLA Ops:
  0.0 0.0 copy-start
  0.0 6.4 stack.11
  6.4 25.1 %all-to-all-start = ((bf16[512,2,16,384]{3,2,1,0:T(8,128)(2,1)}), bf16[512,2,16,384]{3,2,1,0:T(8,128)(2,1)}, u32[]{:S(2)}, u32[]{:S(2)}) async-start(bf16[512,2,16,384]{3,2,1,0:T(8,128)(2,1)} %stack.11), calls=%async_computation | async-start | bytes 25165824 | tf_op jit(solution)/shard_map/all_to_all | solution.py:16
  31.6 0.0 copy-done.2
  31.6 0.1 fusion.14
  31.7 0.1 min.18
  31.8 0.1 min.16
  31.8 0.1 fusion.17
  31.9 0.1 and.18
  32.1 541.1 %all-to-all-done = bf16[512,2,16,384]{3,2,1,0:T(8,128)(2,1)} async-done(((bf16[512,2,16,384]{3,2,1,0:T(8,128)(2,1)}), bf16[512,2,16,384]{3,2,1,0:T(8,128)(2,1)}, u32[]{:S(2)}, u32[]{:S(2)}) %all-to-all-start) | async-done | bytes 12582944 | tf_op jit(solution)/shard_map/all_to_all | solution.py:16
  573.1 7.0 copy.11
  580.1 117.9 %copy.12 = bf16[2,8192,384]{2,0,1:T(2,128)(2,1)} copy(bf16[2,8192,384]{2,1,0:T(8,128)(2,1)S(1)} %bitcast.48) | data formatting | bytes 25165824 | tf_op jit(solution)/shard_map/reshape | solution.py:15
  698.0 1.9 fusion.7
  700.0 5.2 gather_fusion
  705.2 0.1 fusion.10
  705.3 0.5 fusion.13
  705.8 0.5 fusion.12
  706.3 0.5 fusion.5
  706.9 0.5 fusion.6
  707.4 1.7 pad_maximum_fusion
  709.0 5.5 copy.14
  714.5 124.6 %all_to_all.23 = bf16[2,4,384,384]{3,1,0,2:T(4,128)(2,1)S(1)} all-to-all(bf16[2,4,384,384]{3,1,0,2:T(4,128)(2,1)} %copy.14), channel_id=1, replica_groups=mesh['coef'=16,'pair'=32] {'pair'}, dimensions={2} | all-to-all | bytes 4718592 | tf_op jit(solution)/shard_map/all_to_all | solution.py:37
  839.1 1.8 copy.16
  841.0 2.3 fusion.2
  (8 shorter events, 0.0 us)
Async XLA Ops:
  0.0 698.0 %copy-start = (bf16[4,32,8192]{2,1,0:T(8,128)(2,1)S(1)}, bf16[4,32,8192]{2,1,0:T(8,128)(2,1)}, u32[]{:S(2)}) copy-start(bf16[4,32,8192]{2,1,0:T(8,128)(2,1)} %param.4) | copy-start | bytes 6291460
  6.4 25.2 %copy-start.2 = (s32[8]{0:T(128)S(1)}, s32[8]{0:T(128)}, u32[]{:S(2)}) copy-start(s32[8]{0:T(128)} %param.6) | copy-start | bytes 100
  6.4 566.7 %all-to-all-start = ((bf16[512,2,16,384]{3,2,1,0:T(8,128)(2,1)}), bf16[512,2,16,384]{3,2,1,0:T(8,128)(2,1)}, u32[]{:S(2)}, u32[]{:S(2)}) async-start(bf16[512,2,16,384]{3,2,1,0:T(8,128)(2,1)} %stack.11), calls=%async_computation | async-start | bytes 25165824 | tf_op jit(solution)/shard_map/all_to_all | solution.py:16
  839.1 1.8 copy-start.1
